TPU v7x, 32 devices: a whole 2x2x4 slice. The times are simulated.
32 devices in a mesh: ha: 8 (over z, core), wa: 4 (over y, x).
Axes of the slice: x: 2, y: 2, z: 4, core: 2. Of those that a mesh axis runs over, the one named last changes fastest.
Arguments:
- latents: bfloat16 [64, 64, 64, 512], P('ha', 'wa'), may hold values from -8 to 8
- cotangent: bfloat16 [64, 64, 64, 512], P('ha', 'wa'), may hold values from -0.59765625 to 0.59765625
- w_down: bfloat16 [512, 18], replicated, may hold values from -0.25 to 0.25
- bit_bias: float32 [18], replicated, may hold values from -1.5 to 1.5
- w_up: bfloat16 [18, 512], replicated, may hold values from -1.5 to 1.5
Outputs:
- grad_latents: bfloat16 [64, 64, 64, 512], P('ha', 'wa')
- bit_entropy: float32 [64, 64, 64], P('ha', 'wa')
- marginal: float32 [18], replicated
- grad_down: float32 [512, 18], replicated
- grad_bias: float32 [18], replicated
- grad_up: float32 [18, 512], replicated
All inputs are finite; a program needn't handle non-finite values.
Results may differ from a plain program's by a relative error of at most 0.005.
Values may be sent and summed in bfloat16 or wider, within the bound.
No kernel may reach another device: no remote copies, remote signals or barrier semaphores. Data moves between devices by JAX's collectives and lax.ppermute only.
A program may use at most 128 MiB of HBM per device.

v0:
```python
import functools
import math

import jax
import jax.numpy as jnp
from jax import lax
from jax.experimental import pallas as pl
from jax.experimental.pallas import tpu as pltpu
from jax.sharding import PartitionSpec as P


local_weight = 4.0
margin_weight = 4.0
BF, F32 = jnp.bfloat16, jnp.float32
EARLY_ROWS, FIRST_ROWS, AHEAD_ROWS = 4, 6, 2


VMEM = pl.BlockSpec(memory_space=pltpu.VMEM)
HBM = pl.BlockSpec(memory_space=pltpu.HBM)


def params(mib):
    return pltpu.CompilerParams(vmem_limit_bytes=mib * 2**20)


def cost(flops, bytes_accessed):
    return pl.CostEstimate(flops=flops, bytes_accessed=bytes_accessed, transcendentals=0)


def dot(a, b, dims):
    return lax.dot_general(a, b, (dims, ((), ())), preferred_element_type=F32)


def to_column(row, n):
    eye = lax.broadcasted_iota(jnp.int32, (n, n), 0) == lax.broadcasted_iota(jnp.int32, (n, n), 1)
    return jnp.sum(jnp.where(eye, row, 0.0), axis=1, keepdims=True)


def to_row(column, n):
    eye = lax.broadcasted_iota(jnp.int32, (n, n), 0) == lax.broadcasted_iota(jnp.int32, (n, n), 1)
    return jnp.sum(jnp.where(eye, column, 0.0), axis=0, keepdims=True)


def even(axis):
    return lax.rem(lax.axis_index(axis), 2) == 0


def prob_of(squash):
    return 0.01 + 0.98 * squash


def spaced(shape, dtype=F32):
    return jax.ShapeDtypeStruct(shape, dtype)


def border(r, rows):
    return r if r < 2 else r - (rows - 4) if r >= rows - 2 else None


def latent_row(edge_ref, ahead_ref, middle_ref, r, rows):
    k = border(r, rows)
    return edge_ref[k] if k is not None else split_row(ahead_ref, middle_ref, r - 2, ahead_ref.shape[0])


def row_of(edge_ref, middle_ref, r, rows):
    k = border(r, rows)
    return middle_ref[r - 2] if k is None else edge_ref[k]


def split_row(edge_ref, middle_ref, r, count):
    return edge_ref[r] if r < count else middle_ref[r - count]


def logits_of(x, wt, bias):
    return dot(wt, x.reshape(-1, x.shape[-1]), ((1,), (1,))) + bias


def add_mass(mass, squash):
    prob = prob_of(squash)
    for k in range(prob.shape[1] // 128):
        mass += prob[:, k * 128 : (k + 1) * 128]
    return mass


def put_edges(ea_ref, eb_ref, k, logits, edge, wa_even):
    bits, lanes = logits.shape
    left, right = logits[:, :edge].astype(BF), logits[:, lanes - edge :].astype(BF)
    ea_ref[k, :bits] = jnp.where(wa_even, right, left)
    eb_ref[k, :bits] = jnp.where(wa_even, left, right)


def encode_kernel(x_hbm, wt_hbm, bias_hbm, x_ref, sq_ref, ea_ref, eb_ref, ra_ref, rb_ref, mass_ref, wt_ref, bias_ref, ahead_ref, sem):
    rows, bits = x_hbm.shape[0], sq_ref.shape[1]
    edge = 2 * x_hbm.shape[2]
    order = (0, 1, rows - 2, rows - 1, *range(2, 2 + ahead_ref.shape[0]))
    small = [pltpu.make_async_copy(wt_hbm, wt_ref, sem.at[4]), pltpu.make_async_copy(bias_hbm, bias_ref, sem.at[5])]
    place = lambda k: x_ref.at[k] if k < 4 else ahead_ref.at[k - 4]
    copies = [pltpu.make_async_copy(x_hbm.at[r], place(k), sem.at[k if k < 4 else k + 2]) for k, r in enumerate(order)]
    copies, ahead = copies[:4], copies[4:]
    for copy in small + copies + ahead:
        copy.start()
    for copy in small:
        copy.wait()
    wt, bias = wt_ref[...], to_column(bias_ref[...], bits)
    wa_even, ha_even = even("wa"), even("ha")
    mass = jnp.zeros((bits, 128), F32)
    packed = []
    for k, copy in enumerate(copies):
        copy.wait()
        logits = logits_of(x_ref[k], wt, bias)
        squash = jax.nn.sigmoid(logits)
        sq_ref[k] = squash
        mass = add_mass(mass, squash)
        put_edges(ea_ref, eb_ref, k, logits, edge, wa_even)
        packed.append(logits.astype(BF))
        if k >= 2:
            ra_ref[k - 2, :bits] = jnp.where(ha_even, packed[k], packed[k - 2])
            rb_ref[k - 2, :bits] = jnp.where(ha_even, packed[k - 2], packed[k])
    mass_ref[...] = mass
    for copy in ahead:
        copy.wait()


def encode(latents, wt, bit_bias, padded, ahead):
    _, cols, images, width = latents.shape
    bits = wt.shape[0]
    lanes, edge = cols * images, 2 * images
    return pl.pallas_call(
        encode_kernel,
        in_specs=[HBM] * 3,
        out_specs=[VMEM] * 10,
        out_shape=[
            pltpu.VMEM((4, cols, images, width), BF),
            spaced((4, bits, lanes)),
            spaced((4, padded, edge), BF),
            spaced((4, padded, edge), BF),
            spaced((2, padded, lanes), BF),
            spaced((2, padded, lanes), BF),
            spaced((bits, 128)),
            spaced(wt.shape, BF),
            spaced(bit_bias.shape),
            pltpu.VMEM((ahead, cols, images, width), BF),
        ],
        scratch_shapes=[pltpu.SemaphoreType.DMA((6 + ahead,))],
        compiler_params=params(8),
        cost_estimate=cost(2 * 4 * lanes * width * 256, 4 * lanes * width * 2),
        name="encode",
    )(latents, wt, bit_bias)


def outward_row(x, w, squash, total):
    x = x.reshape(-1, x.shape[-1])
    code = (2.0 * squash - 1.0).astype(BF)
    return dot(w, x, ((1,), (1,))), total + dot(code, x, ((1,), (0,)))


def middle_kernel(
    x_hbm, c_hbm, wt_ref, bias_ref, up_w_ref, sqe_ref, mass_in, xa_ref,
    x_ref, sq_ref, ea_ref, eb_ref, mass_ref, cg_ref, up_ref,
    c_ref, sem,
):
    rows, (inside, bits, lanes), early = x_hbm.shape[0], sq_ref.shape, cg_ref.shape[0]
    edge = 2 * x_hbm.shape[2]
    ahead = xa_ref.shape[0]
    copies = [pltpu.make_async_copy(x_hbm.at[2 + k], x_ref.at[k - ahead], sem.at[k]) for k in range(ahead, inside)]
    outward = [pltpu.make_async_copy(c_hbm.at[k], c_ref.at[k], sem.at[inside + k]) for k in range(early)]
    for copy in copies + outward:
        copy.start()
    wt, bias = wt_ref[...], to_column(bias_ref[...], bits)
    wa_even = even("wa")
    mass = mass_in[...]
    for k in range(inside):
        if k >= ahead:
            copies[k - ahead].wait()
        logits = logits_of(split_row(xa_ref, x_ref, k, ahead), wt, bias)
        squash = jax.nn.sigmoid(logits)
        sq_ref[k] = squash
        mass = add_mass(mass, squash)
        put_edges(ea_ref, eb_ref, k, logits, edge, wa_even)
    row = to_row(jnp.sum(mass, axis=1, keepdims=True), bits)
    mass_ref[...] = jnp.concatenate([row, jnp.zeros((1, 128 - bits), F32)], axis=1)
    total = jnp.zeros(up_ref.shape, F32)
    for k, copy in enumerate(outward):
        copy.wait()
        cg_ref[k], total = outward_row(c_ref[k], up_w_ref[...], row_of(sqe_ref, sq_ref, k, rows), total)
    up_ref[...] = total


def middle(latents, cotangent, wt, bias, w_up, squash, mass, x_ahead, padded, early):
    rows, cols, images, width = latents.shape
    bits, lanes, edge = wt.shape[0], cols * images, 2 * images
    inside = rows - 4
    return pl.pallas_call(
        middle_kernel,
        in_specs=[HBM] * 2 + [VMEM] * 6,
        out_specs=[VMEM] * 7,
        out_shape=[
            pltpu.VMEM((inside - x_ahead.shape[0], cols, images, width), BF),
            spaced((inside, bits, lanes)),
            spaced((inside, padded, edge), BF),
            spaced((inside, padded, edge), BF),
            spaced((1, 128)),
            spaced((early, bits, lanes)),
            spaced((bits, width)),
        ],
        scratch_shapes=[pltpu.VMEM((early, cols, images, width), BF), pltpu.SemaphoreType.DMA((inside + early,))],
        compiler_params=params(12),
        cost_estimate=cost(2 * (inside + 2 * early) * lanes * width * 256, (inside + early) * lanes * width * 2),
        name="middle",
    )(latents, cotangent, wt, bias, w_up, squash, mass, x_ahead)


def heights(bits, count):
    main = bits // 8 * 8
    return main, count * main, -(-count * (bits - main) // 8) * 8


def unpack(ref, k, bits, count):
    main, at, spare = heights(bits, count)
    body = ref[k * main : (k + 1) * main].astype(F32)
    if not spare:
        return body
    left = bits - main
    return jnp.concatenate([body, ref[at : at + spare].astype(F32)[k * left : (k + 1) * left]], axis=0)


def pack_kernel(bits, ea_e, eb_e, ea_m, eb_m, ha_a, ha_b, mass_ref, ea_ref, eb_ref):
    rows, edge = ea_e.shape[0] + ea_m.shape[0], ea_ref.shape[1]
    lanes = ha_a.shape[2]
    main, at, spare = heights(bits, rows + 4)
    wa_even, ha_even = even("wa"), even("ha")
    above, below = [], []
    for k in range(2):
        above.append(jnp.where(ha_even, ha_b[k], ha_a[k]))
        below.append(jnp.where(ha_even, ha_a[k], ha_b[k]))
    row = mass_ref[...]
    high = row.astype(BF).astype(F32)
    middle = (row - high).astype(BF).astype(F32)
    parts = jnp.concatenate([high, middle, row - high - middle, jnp.zeros((5, edge), F32)], axis=0)
    for out, outer, inner, take_right in ((ea_ref, ea_e, ea_m, wa_even), (eb_ref, eb_e, eb_m, jnp.logical_not(wa_even))):
        pick = lambda side: jnp.where(take_right, side[:, lanes - edge :], side[:, :edge])
        values = [*map(pick, above), outer[0], outer[1], *[inner[k] for k in range(rows - 4)], outer[2], outer[3], *map(pick, below)]
        for e, value in enumerate(values):
            out[e * main : (e + 1) * main] = value[:main]
        if spare:
            unused = spare - (bits - main) * len(values)
            left = [value.astype(F32)[main:bits] for value in values] + [jnp.zeros((unused, edge), F32)] * (unused > 0)
            out[at : at + spare] = jnp.concatenate(left, axis=0).astype(BF)
        out[at + spare :] = parts.astype(BF)


def pack(edges, halos, mass, rows, bits):
    edge = edges[0].shape[2]
    _, at, spare = heights(bits, rows + 4)
    return pl.pallas_call(
        functools.partial(pack_kernel, bits),
        in_specs=[VMEM] * 7,
        out_specs=[VMEM] * 2,
        out_shape=[spaced((at + spare + 8, edge), BF)] * 2,
        compiler_params=params(2),
        cost_estimate=cost(0, 2**18),
        name="pack",
    )(*edges, *halos, mass)


def window(t, cell):
    wide = t.shape[1] - 2 * cell
    return (t[:, :wide] + t[:, cell : cell + wide] + t[:, 2 * cell :]) / 9.0


def slope_of(t, cell):
    pooled = window(t, cell)
    lp, lq = jnp.log(pooled), jnp.log(1.0 - pooled)
    return local_weight * (lq - lp), jnp.sum(pooled * (lq - lp) - lq, axis=0, keepdims=True)


def gradients(t, cell, squash, cg, stacked):
    bits, lanes = squash.shape
    half = stacked.shape[0] // 2
    steep = squash * (1.0 - squash)
    g = 2.0 * cg + 0.98 * window(t, cell)
    stacked[:bits] = (g * steep).astype(BF)
    stacked[half : half + bits] = steep.astype(BF)
    values = stacked[...]
    columns = values[:, :128].astype(F32)
    for k in range(1, lanes // 128):
        columns += values[:, k * 128 : (k + 1) * 128].astype(F32)
    return g, values, columns


def inner_kernel(
    c_hbm, xe_ref, xa_ref, xm_ref, sqe_ref, sqm_ref, ha_a, ha_b, cg_in, up_in, up_w_ref, after,
    cg_ref, up_ref, g_ref, slope_ref, ent_ref, acc_ref, columns_ref, pe_ref,
    c_ref, stacked, sem,
):
    late, bits, lanes = cg_ref.shape
    early, rows = cg_in.shape[0], g_ref.shape[0]
    images, width = xe_ref.shape[2:]
    edge = 2 * images
    copies = [pltpu.make_async_copy(c_hbm.at[early + k], c_ref.at[k], sem.at[k]) for k in range(late)]
    for copy in copies:
        copy.start()
    ha_even = even("ha")
    stacked[...] = jnp.zeros_like(stacked)
    for k in range(2):
        a, b = ha_a[k, :bits], ha_b[k, :bits]
        pe_ref[k] = prob_of(jax.nn.sigmoid(jnp.where(ha_even, b, a).astype(F32)))
        pe_ref[rows + 2 + k] = prob_of(jax.nn.sigmoid(jnp.where(ha_even, a, b).astype(F32)))
    for r in range(rows):
        pe_ref[2 + r] = prob_of(row_of(sqe_ref, sqm_ref, r, rows))
    def slope_row(e):
        slope_ref[e], entropy = slope_of(pe_ref[e] + pe_ref[e + 1] + pe_ref[e + 2], images)
        if 1 <= e <= rows:
            ent_ref[e - 1 : e] = entropy

    slope_row(0)
    slope_row(1)
    total = up_in[...]
    acc = jnp.zeros(acc_ref.shape, F32)
    columns = jnp.zeros(columns_ref.shape, F32)
    for r in range(rows):
        squash = row_of(sqe_ref, sqm_ref, r, rows)
        if r < early:
            cg = cg_in[r]
        else:
            copies[r - early].wait()
            cg, total = outward_row(c_ref[r - early], up_w_ref[...], squash, total)
            cg_ref[r - early] = cg
        slope_row(r + 2)
        t = slope_ref[r] + slope_ref[r + 1] + slope_ref[r + 2]
        g_ref[r], values, sums = gradients(t, images, squash[:, edge : lanes - edge], cg[:, edge : lanes - edge], stacked.at[r % 2])
        x = latent_row(xe_ref, xa_ref, xm_ref, r, rows)[2:-2].reshape(lanes - 2 * edge, width)
        acc += dot(values, x, ((1,), (0,)))
        columns += sums
    acc_ref[...] = acc
    columns_ref[...] = columns
    up_ref[...] = total


def inner(cotangent, x_edge, x_ahead, x_middle, sq_edge, sq_middle, ha_a, ha_b, cg, up, w_up, after):
    rows, cols, images, width = cotangent.shape
    early, bits, lanes = cg.shape
    late, edge = rows - early, 2 * images
    padded = -(-bits // 16) * 16
    return pl.pallas_call(
        inner_kernel,
        in_specs=[HBM] + [VMEM] * 10 + [pl.BlockSpec(memory_space=pl.ANY)],
        out_specs=[VMEM] * 8,
        out_shape=[
            spaced((late, bits, lanes)),
            spaced((bits, width)),
            spaced((rows, bits, lanes - 2 * edge)),
            spaced((rows + 2, bits, lanes - edge)),
            spaced((rows, lanes - edge)),
            spaced((2 * padded, width)),
            spaced((2 * padded, 128)),
            spaced((rows + 4, bits, lanes)),
        ],
        scratch_shapes=[
            pltpu.VMEM((late, cols, images, width), BF),
            pltpu.VMEM((2, 2 * padded, lanes - 2 * edge), BF),
            pltpu.SemaphoreType.DMA((late,)),
        ],
        compiler_params=params(12),
        cost_estimate=cost(2 * (2 * late + rows) * lanes * width * 256, late * lanes * width * 2),
        name="inner",
    )(cotangent, x_edge, x_ahead, x_middle, sq_edge, sq_middle, ha_a, ha_b, cg, up, w_up, after)


def outer_kernel(
    xe_ref, xa_ref, xm_ref, sqe_ref, sqm_ref, cg0_ref, cg1_ref, wa_a, wa_b, slope_ref, pe_ref, acc_in, columns_in, up_ref, mass_ref,
    g_ref, ent_ref, mine_ref, other_ref,
    near, stacked,
):
    rows, bits, _ = g_ref.shape
    images, width = xe_ref.shape[2:]
    lanes, edge = sqe_ref.shape[2], 2 * images
    half = stacked.shape[1] // 2
    wa_even, ha_even = even("wa"), even("ha")
    stacked[...] = jnp.zeros_like(stacked)
    ends = lambda v: jnp.concatenate([v[:, :edge], v[:, lanes - edge :]], axis=1)
    probs = []
    for e in range(rows + 4):
        a, b = unpack(wa_a, e, bits, rows + 4), unpack(wa_b, e, bits, rows + 4)
        left = prob_of(jax.nn.sigmoid(jnp.where(wa_even, b, a)))
        right = prob_of(jax.nn.sigmoid(jnp.where(wa_even, a, b)))
        own = pe_ref[e]
        probs.append((jnp.concatenate([left, own[:, :edge]], axis=1), jnp.concatenate([own[:, lanes - edge :], right], axis=1)))
    for e in range(rows + 2):
        sides = [probs[e][i] + probs[e + 1][i] + probs[e + 2][i] for i in range(2)]
        (left, left_ent), (right, right_ent) = [slope_of(t, images) for t in sides]
        if 1 <= e <= rows:
            ent_ref[e - 1 : e] = jnp.concatenate([left_ent[:, images:], right_ent[:, :images]], axis=1)
        inside = slope_ref[e]
        near[e, 0] = jnp.concatenate([left, inside[:, :edge]], axis=1)
        near[e, 1] = jnp.concatenate([inside[:, lanes - 2 * edge :], right], axis=1)
    acc, columns = acc_in[...], columns_in[...]
    for r in range(rows):
        squash, cg = ends(row_of(sqe_ref, sqm_ref, r, rows)), ends(split_row(cg0_ref, cg1_ref, r, cg0_ref.shape[0]))
        x = latent_row(xe_ref, xa_ref, xm_ref, r, rows)
        x = jnp.concatenate([x[:2].reshape(edge, width), x[-2:].reshape(edge, width)], axis=0)
        spread = jnp.concatenate([window(near[r, i] + near[r + 1, i] + near[r + 2, i], images) for i in range(2)], axis=1)
        steep = squash * (1.0 - squash)
        g = 2.0 * cg + 0.98 * spread
        g_ref[r] = g
        at = stacked.at[r % 2]
        at[:bits] = (g * steep).astype(BF)
        at[half : half + bits] = steep.astype(BF)
        values = at[...]
        acc += dot(values, x, ((1,), (0,)))
        for k in range(2 * edge // 128):
            columns += values[:, k * 128 : (k + 1) * 128].astype(F32)
    total = jnp.sum(columns, axis=1, keepdims=True)
    others = sum(ref[ref.shape[0] - 8 :].astype(F32)[k : k + 1] for ref in (wa_a, wa_b) for k in range(3))
    rows_of = (to_row(total[:bits], bits), to_row(total[half : half + bits], bits), mass_ref[:, :bits], others[:, :bits])
    low, high = slice(0, width // 2), slice(width // 2, width)
    pieces = ((0, acc[:bits]), (bits, acc[half : half + bits]), (2 * bits, up_ref[...]))
    lead = 3 * bits
    for ref, flip in ((mine_ref, False), (other_ref, True)):
        ref[lead:, :] = jnp.zeros((ref.shape[0] - lead, ref.shape[1]), F32)
        take_low = jnp.logical_xor(ha_even, flip)
        for at, piece in pieces:
            ref[at : at + bits] = jnp.where(take_low, piece[:, low], piece[:, high])
        ref[lead : lead + 1, :bits] = rows_of[0]
        ref[lead : lead + 1, 128 : 128 + bits] = rows_of[1]
        ref[lead + 1 : lead + 2, :bits] = rows_of[2]
        ref[lead + 1 : lead + 2, 128 : 128 + bits] = rows_of[3]


def outer(rows, width, images, *operands):
    bits = operands[3].shape[1]
    padded = -(-bits // 16) * 16
    sums = -(-(3 * bits + 2) // 8) * 8
    edge = 2 * images
    return pl.pallas_call(
        outer_kernel,
        in_specs=[VMEM] * len(operands),
        out_specs=[VMEM] * 4,
        out_shape=[spaced((rows, bits, 2 * edge)), spaced((rows, edge)), spaced((sums, width // 2)), spaced((sums, width // 2))],
        scratch_shapes=[pltpu.VMEM((rows + 2, 2, bits, 2 * edge), F32), pltpu.VMEM((2, 2 * padded, 2 * edge), BF)],
        compiler_params=params(8),
        cost_estimate=cost(2 * rows * 2 * edge * width * 256, 2**20),
        name="outer",
    )(*operands)


def back_kernel(count, slots, gi_ref, go_ref, sqe_ref, sqm_ref, wt_ref, *refs):
    sums = refs[: len(slots)]
    ei_ref, eo_ref, out_hbm, ent_hbm, rest_ref, out_ref, sem, ent_ref, ent_sem = refs[len(slots) :]
    rows, bits, edge = go_ref.shape
    edge //= 2
    cols, images = ent_ref.shape[1:]
    for c in range(cols):
        at = (c - 1) * images
        ent_ref[:, c, :] = eo_ref[:, :images] if c == 0 else eo_ref[:, images:] if c == cols - 1 else ei_ref[:, at : at + images]
    entropy_copy = pltpu.make_async_copy(ent_ref, ent_hbm, ent_sem)
    entropy_copy.start()
    at = 3 * bits + 1
    marginal = sum(ref[at : at + 1, lane : lane + bits] for ref, lane in zip(sums, slots)) / count
    drift = to_column(0.98 * margin_weight * jnp.log((1.0 - marginal) / marginal), bits)
    wt = wt_ref[...]
    first = out_ref.shape[0]
    copies = [pltpu.make_async_copy(out_ref.at[r], out_hbm.at[r], sem.at[r]) for r in range(first)]
    for r in range(rows):
        squash = row_of(sqe_ref, sqm_ref, r, rows)
        g = jnp.concatenate([go_ref[r][:, :edge], gi_ref[r], go_ref[r][:, edge:]], axis=1)
        grad = ((g - drift) * (squash * (1.0 - squash))).astype(BF)
        value = dot(grad, wt, ((0,), (0,))).astype(BF).reshape(out_ref.shape[1:])
        if r < first:
            out_ref[r] = value
            copies[r].start()
        else:
            rest_ref[r - first] = value
    for copy in copies + [entropy_copy]:
        copy.wait()


def back(shape, g_inner, g_outer, sq_edge, sq_middle, wt, marginal, count, first, ent_inner, ent_outer):
    arrays, slots = zip(*marginal)
    operands = [g_inner, g_outer, sq_edge, sq_middle, wt, *arrays, ent_inner, ent_outer]
    cells = math.prod(shape)
    return pl.pallas_call(
        functools.partial(back_kernel, count, slots),
        in_specs=[VMEM] * len(operands),
        out_specs=[HBM, HBM, VMEM],
        out_shape=[spaced(shape, BF), spaced(shape[:3]), pltpu.VMEM((shape[0] - first, *shape[1:]), BF)],
        scratch_shapes=[
            pltpu.VMEM((first, *shape[1:]), BF),
            pltpu.SemaphoreType.DMA((first,)),
            pltpu.VMEM(shape[:3], F32),
            pltpu.SemaphoreType.DMA,
        ],
        compiler_params=params(16),
        cost_estimate=cost(2 * cells * 256, cells * 2),
        name="back",
    )(*operands)


def store_kernel(rest_ref, _, out_hbm, sem):
    count = rest_ref.shape[0]
    first = out_hbm.shape[0] - count
    copies = [pltpu.make_async_copy(rest_ref.at[k], out_hbm.at[first + k], sem.at[k]) for k in range(count)]
    for copy in copies:
        copy.start()
    for copy in copies:
        copy.wait()


def store(rest, onto):
    return pl.pallas_call(
        store_kernel,
        in_specs=[VMEM, HBM],
        out_specs=HBM,
        out_shape=spaced(onto.shape, BF),
        input_output_aliases={1: 0},
        scratch_shapes=[pltpu.SemaphoreType.DMA((rest.shape[0],))],
        compiler_params=params(2),
        cost_estimate=cost(0, rest.size * 2),
        name="store",
    )(rest, onto)


def finish_kernel(count, mine_ref, other_ref, marginal_ref, down_ref, bias_ref, up_ref):
    bits = marginal_ref.shape[1]
    core = even("ha")
    a, b = mine_ref[...], other_ref[...]
    sums = jnp.concatenate([jnp.where(core, a, b), jnp.where(core, b, a)], axis=1)
    mass = mine_ref[3 * bits + 1 : 3 * bits + 2, :bits]
    marginal = mass / count
    marginal_ref[...] = marginal
    drift_row = margin_weight * jnp.log((1.0 - marginal) / marginal)
    drift = to_column(drift_row, bits)
    down = (sums[:bits] - 0.98 * drift * sums[bits : 2 * bits]) / count
    down_ref[...] = down
    bias_ref[...] = (mine_ref[3 * bits : 3 * bits + 1, :bits] - 0.98 * drift_row * mine_ref[3 * bits : 3 * bits + 1, 128 : 128 + bits]) / count
    up_ref[...] = sums[2 * bits : 3 * bits] / count


def finish(mine, other, bits, count):
    width = 2 * mine.shape[1]
    return pl.pallas_call(
        functools.partial(finish_kernel, count),
        out_shape=[
            jax.ShapeDtypeStruct((1, bits), F32),
            jax.ShapeDtypeStruct((bits, width), F32),
            jax.ShapeDtypeStruct((1, bits), F32),
            jax.ShapeDtypeStruct((bits, width), F32),
        ],
        compiler_params=pltpu.CompilerParams(vmem_limit_bytes=8 * 2**20),
        name="finish",
    )(mine, other)


def swap(x, axis, mask):
    return lax.ppermute(x, axis, [(i, i ^ mask) for i in range(lax.axis_size(axis))])


def swap_outer(x, axis):
    count = lax.axis_size(axis)
    return lax.ppermute(x, axis, [(i, (((i + 1) ^ 1) - 1) % count) for i in range(count)])


def exchanged(x, axis, stride, radix):
    return [swap(x, axis, d * stride) for d in ((3, 1, 2) if radix == 4 else (1,))]


def stages(count, stride):
    while stride < count:
        radix = 4 if stride * 4 <= count else 2
        yield stride, radix
        stride *= radix


def summed(x, axis, start):
    for stride, radix in stages(lax.axis_size(axis), start):
        x = sum(exchanged(x, axis, stride, radix), x)
    return x


def local(latents, cotangent, w_down, bit_bias, w_up):
    rows, cols, images, width = latents.shape
    bits = w_down.shape[1]
    columns = lax.axis_size("wa")
    count = rows * cols * images * lax.axis_size("ha") * columns
    padded = -(-bits // 8) * 8
    early, first = EARLY_ROWS, FIRST_ROWS
    near = lambda a: pltpu.with_memory_space_constraint(a, pltpu.HBM)
    resident = lambda a: pltpu.with_memory_space_constraint(a, pltpu.VMEM)
    latents, cotangent = near(latents), near(cotangent)
    x_e, sq_e, ea_e, eb_e, ra, rb, mass, wt, bias, x_a = encode(latents, near(w_down.T), near(bit_bias.reshape(1, bits)), padded, AHEAD_ROWS)
    ha_b = swap_outer(rb, "ha")
    ha_a = swap(ra, "ha", 1)
    x_m, sq_m, ea_m, eb_m, mass, cg0, up = middle(latents, cotangent, wt, bias, w_up, sq_e, mass, resident(x_a), padded, early)
    x_e, x_a, x_m = resident(x_e), resident(x_a), resident(x_m)
    ea, eb = pack((ea_e, eb_e, ea_m, eb_m), (ha_a, ha_b), mass, rows, bits)
    wa_a, wa_b = swap(ea, "wa", 1), swap_outer(eb, "wa")
    cg1, up, g_inner, slope, ent_inner, acc, sums, probs = inner(cotangent, x_e, x_a, x_m, sq_e, sq_m, ha_a, ha_b, cg0, up, w_up, ea)
    g_outer, ent_outer, mine, other = outer(
        rows, width, images, x_e, x_a, x_m, sq_e, sq_m, cg0, cg1, wa_a, wa_b, slope, probs, acc, sums, up, mass
    )
    sums = mine + swap(other, "ha", 1)
    sums = summed(sums, "ha", 2)
    run = functools.partial(back, latents.shape, g_inner, g_outer, sq_e, sq_m, wt)
    if columns == 4:
        opposite, *rest = [swap(sums, "wa", d) for d in (2, 1, 3)]
        known = [(sums, 0), (sums, 128), (opposite, 0)]
        grad_latents, entropy, rest_rows = run(known, count, first, ent_inner, ent_outer)
        near_sums, grad_latents = lax.optimization_barrier((sums + opposite, grad_latents))
        sums = sum(rest, near_sums)
    else:
        sums = summed(sums, "wa", 1)
        grad_latents, entropy, rest_rows = run([(sums, 0)], count, first, ent_inner, ent_outer)
    partner = swap(sums, "ha", 1)
    grad_latents = store(rest_rows, grad_latents)
    marginal, grad_down, grad_bias, grad_up = finish(sums, partner, bits, count)
    return grad_latents, entropy, marginal.reshape(bits), grad_down.T, grad_bias.reshape(bits), grad_up


def solution(mesh):
    placed = (P("ha", "wa", None, None), P("ha", "wa", None, None), P(), P(), P())
    return jax.shard_map(
        local,
        mesh=mesh,
        in_specs=placed,
        out_specs=(P("ha", "wa", None, None), P("ha", "wa", None), P(), P(), P(), P()),
        check_vma=False,
    )
```

profile of v0, /device:TPU:0, one launch (start us, length us, event | category | flops | bytes accessed | tf_op | source)
XLA Modules:
  0.0 40.1 jit_solution(13494078745246533997)
XLA Ops:
  0.6 3.1 %encode.1 = (bf16[4,16,64,512]{3,2,1,0:T(8,128)(2,1)S(1)}, f32[4,18,1024]{2,1,0:T(8,128)S(1)}, bf16[4,24,128]{2,1,0:T(8,128)(2,1)S(1)}, bf16[4,24,128]{2,1,0:T(8...) custom-call(bf16[8,16,64,512]{3,2,1,0:T(8,128)(2,1)} %x_hbm.3, ...), custom_call_target="tpu_custom_call" | custom-call | flops 1073741824 | bytes 4194304 | tf_op jit(solution)/shard_map/encode/pallas_call | solution.py:128
  3.7 0.6 %collective-permute-start = (bf16[2,24,1024]{2,1,0:T(8,128)(2,1)S(1)}, bf16[2,24,1024]{2,1,0:T(8,128)(2,1)S(1)}, u32[]{:S(2)}, u32[]{:S(2)}) collective-permute-start(bf16[2,24,1024]{2,1,0:T(8,128)(2,1)S(1)} %get-tuple-element.54), channel_id=1, source_target_pairs={{0,4},{4,0},{8,12},{12,8},{16,20},{20,16},{24,28},{28,24},{1,5},{5... | collective-permute-start | bytes 294920 | tf_op jit(solution)/shard_map/ppermute | solution.py:555
  4.3 4.7 %collective-permute-start.1 = (bf16[2,24,1024]{2,1,0:T(8,128)(2,1)S(1)}, bf16[2,24,1024]{2,1,0:T(8,128)(2,1)S(1)}, u32[]{:S(2)}, u32[]{:S(2)}) collective-permute-start(bf16[2,24,1024]{2,1,0:T(8,128)(2,1)S(1)} %get-tuple-element.55), channel_id=1, source_target_pairs={{0,28},{4,8},{8,4},{12,16},{16,12},{20,24},{24,20},{28,0},{1,29},{... | collective-permute-start | bytes 294920 | tf_op jit(solution)/shard_map/ppermute | solution.py:560
  9.0 4.4 %middle.1 = (bf16[2,16,64,512]{3,2,1,0:T(8,128)(2,1)S(1)}, f32[4,18,1024]{2,1,0:T(8,128)S(1)}, bf16[4,24,128]{2,1,0:T(8,128)(2,1)S(1)}, bf16[4,24,128]{2,1,0:T(8...) custom-call(bf16[8,16,64,512]{3,2,1,0:T(8,128)(2,1)} %x_hbm.3, ...), custom_call_target="tpu_custom_call" | custom-call | flops 3221225472 | bytes 8388608 | tf_op jit(solution)/shard_map/middle/pallas_call | solution.py:193
  13.4 0.0 collective-permute-done.1.ha_b
  13.5 2.5 %collective-permute-start.3 = (bf16[224,128]{1,0:T(8,128)(2,1)S(1)}, bf16[224,128]{1,0:T(8,128)(2,1)S(1)}, u32[]{:S(2)}, u32[]{:S(2)}) collective-permute-start(bf16[224,128]{1,0:T(8,128)(2,1)S(1)} %get-tuple-element.66), channel_id=1, source_target_pairs={{0,3},{1,2},{2,1},{3,0},{4,7},{5,6},{6,5},{7,4},{8,11},{9,10},{10,... | collective-permute-start | bytes 172040 | tf_op jit(solution)/shard_map/ppermute | solution.py:560
  16.0 0.5 %collective-permute-start.2 = (bf16[224,128]{1,0:T(8,128)(2,1)S(1)}, bf16[224,128]{1,0:T(8,128)(2,1)S(1)}, u32[]{:S(2)}, u32[]{:S(2)}) collective-permute-start(bf16[224,128]{1,0:T(8,128)(2,1)S(1)} %get-tuple-element.63.after), channel_id=1, source_target_pairs={{0,1},{1,0},{2,3},{3,2},{4,5},{5,4},{6,7},{7,6},{8,9},{9,8},{10,11... | collective-permute-start | bytes 172040 | tf_op jit(solution)/shard_map/ppermute | solution.py:555
  16.5 4.1 %inner.1 = (f32[4,18,1024]{2,1,0:T(8,128)S(1)}, f32[18,512]{1,0:T(8,128)S(1)}, f32[8,18,768]{2,1,0:T(8,128)S(1)}, f32[10,18,896]{2,1,0:T(8,128)S(1)}, f32[8,896]...) custom-call(bf16[8,16,64,512]{3,2,1,0:T(8,128)(2,1)} %c_hbm.3, ...), custom_call_target="tpu_custom_call" | custom-call | flops 4294967296 | bytes 4194304 | tf_op jit(solution)/shard_map/inner/pallas_call | solution.py:345
  20.6 0.8 %outer.1 = (f32[8,18,256]{2,1,0:T(8,128)S(1)}, f32[8,128]{1,0:T(8,128)S(1)}, f32[56,256]{1,0:T(8,128)S(1)}, f32[56,256]{1,0:T(8,128)S(1)}) custom-call(bf16[4,16,64,512]{3,2,1,0:T(8,128)(2,1)S(1)} %get-tuple-element.46.xe_ref, bf16[2,16,64,512]{3,2,1,0:T(8,128)(2,1)S(1)} %get-tuple-element.47.xa_ref, bf16[2,16,64,512]{3,2,1,0:T(8,128)(2,1)S(1)} %get-tuple-element.52.xm_ref, ...), custom_call_target="tpu_custom_call" | custom-call | flops 536870912 | bytes 1048576 | tf_op jit(solution)/shard_map/outer/pallas_call | solution.py:435
  21.5 0.1 collective-permute-start.4
  21.6 1.2 %collective-permute-done.4 = f32[56,256]{1,0:T(8,128)S(1)} collective-permute-done((f32[56,256]{1,0:T(8,128)S(1)}, f32[56,256]{1,0:T(8,128)S(1)}, u32[]{:S(2)}, u32[]{:S(2)}) %collective-permute-start.4) | collective-permute-done | bytes 57376 | tf_op jit(solution)/shard_map/ppermute | solution.py:555
  22.8 0.1 collective-permute-start.7
  22.9 1.4 %collective-permute-start.6 = (f32[56,256]{1,0:T(8,128)S(1)}, f32[56,256]{1,0:T(8,128)S(1)}, u32[]{:S(2)}, u32[]{:S(2)}) collective-permute-start(f32[56,256]{1,0:T(8,128)S(1)} %add.21), channel_id=1, source_target_pairs={{0,8},{4,12},{8,0},{12,4},{16,24},{20,28},{24,16},{28,20},{1,9},{5... | collective-permute-start | bytes 172040 | tf_op jit(solution)/shard_map/ppermute | solution.py:555
  24.2 3.0 %collective-permute-start.5 = (f32[56,256]{1,0:T(8,128)S(1)}, f32[56,256]{1,0:T(8,128)S(1)}, u32[]{:S(2)}, u32[]{:S(2)}) collective-permute-start(f32[56,256]{1,0:T(8,128)S(1)} %add.21), channel_id=1, source_target_pairs={{0,24},{4,28},{8,16},{12,20},{16,8},{20,12},{24,0},{28,4},{1,25},{... | collective-permute-start | bytes 172040 | tf_op jit(solution)/shard_map/ppermute | solution.py:555
  27.2 1.1 %collective-permute-done.7 = f32[56,256]{1,0:T(8,128)S(1)} collective-permute-done((f32[56,256]{1,0:T(8,128)S(1)}, f32[56,256]{1,0:T(8,128)S(1)}, u32[]{:S(2)}, u32[]{:S(2)}) %collective-permute-start.7) | collective-permute-done | bytes 57376 | tf_op jit(solution)/shard_map/ppermute | solution.py:555
  28.3 2.0 %collective-permute-done.5 = f32[56,256]{1,0:T(8,128)S(1)} collective-permute-done((f32[56,256]{1,0:T(8,128)S(1)}, f32[56,256]{1,0:T(8,128)S(1)}, u32[]{:S(2)}, u32[]{:S(2)}) %collective-permute-start.5) | collective-permute-done | bytes 57376 | tf_op jit(solution)/shard_map/ppermute | solution.py:555
  30.3 0.6 %collective-permute-start.8 = (f32[56,256]{1,0:T(8,128)S(1)}, f32[56,256]{1,0:T(8,128)S(1)}, u32[]{:S(2)}, u32[]{:S(2)}) collective-permute-start(f32[56,256]{1,0:T(8,128)S(1)} %add_add_fusion.1.refs_0_.refs_1_), channel_id=1, source_target_pairs={{0,2},{1,3},{2,0},{3,1},{4,6},{5,7},{6,4},{7,5},{8,10},{9,11},{10,... | collective-permute-start | bytes 172040 | tf_op jit(solution)/shard_map/ppermute | solution.py:555
  30.9 2.4 %collective-permute-start.10 = (f32[56,256]{1,0:T(8,128)S(1)}, f32[56,256]{1,0:T(8,128)S(1)}, u32[]{:S(2)}, u32[]{:S(2)}) collective-permute-start(f32[56,256]{1,0:T(8,128)S(1)} %add_add_fusion.1.refs_0_.refs_1_), channel_id=1, source_target_pairs={{0,3},{1,2},{2,1},{3,0},{4,7},{5,6},{6,5},{7,4},{8,11},{9,10},{10,... | collective-permute-start | bytes 172040 | tf_op jit(solution)/shard_map/ppermute | solution.py:555
  33.3 0.5 %collective-permute-start.9 = (f32[56,256]{1,0:T(8,128)S(1)}, f32[56,256]{1,0:T(8,128)S(1)}, u32[]{:S(2)}, u32[]{:S(2)}) collective-permute-start(f32[56,256]{1,0:T(8,128)S(1)} %add_add_fusion.1.refs_0_.refs_1_), channel_id=1, source_target_pairs={{0,1},{1,0},{2,3},{3,2},{4,5},{5,4},{6,7},{7,6},{8,9},{9,8},{10,11... | collective-permute-start | bytes 172040 | tf_op jit(solution)/shard_map/ppermute | solution.py:555
  33.9 0.7 %collective-permute-done.8.refs_2_ = f32[56,256]{1,0:T(8,128)S(1)} collective-permute-done((f32[56,256]{1,0:T(8,128)S(1)}, f32[56,256]{1,0:T(8,128)S(1)}, u32[]{:S(2)}, u32[]{:S(2)}) %collective-permute-start.8) | collective-permute-done | bytes 57376 | tf_op jit(solution)/shard_map/ppermute | solution.py:555
  34.6 3.3 %back.1 = (bf16[8,16,64,512]{3,2,1,0:T(8,128)(2,1)}, f32[8,16,64]{2,1,0:T(8,128)}, bf16[2,16,64,512]{3,2,1,0:T(8,128)(2,1)S(1)}) custom-call(f32[8,18,768]{2,1,0:T(8,128)S(1)} %get-tuple-element.64.gi_ref, f32[8,18,256]{2,1,0:T(8,128)S(1)} %get-tuple-element.72.go_ref, f32[4,18,1024]{2,1,0:T(8,128)S(1)} %get-tuple-element.50.sqe_ref, ...), custom_call_target="tpu_custom_call" | custom-call | flops 2147483648 | bytes 8388608 | tf_op jit(solution)/shard_map/back/pallas_call | solution.py:482
  38.0 0.1 collective-permute-start.11
  38.0 1.3 %store.1 = bf16[8,16,64,512]{3,2,1,0:T(8,128)(2,1)} custom-call(bf16[2,16,64,512]{3,2,1,0:T(8,128)(2,1)S(1)} %get-tuple-element.77.rest_ref, bf16[8,16,64,512]{3,2,1,0:T(8,128)(2,1)} %get-tuple-element.79._), custom_call_target="tpu_custom_call", output_to_operand_aliasing={{}: (1, {})} | custom-call | bytes 2097152 | tf_op jit(solution)/shard_map/store/pallas_call | solution.py:510
  39.4 0.7 %finish.1 = (f32[1,18]{1,0:T(1,128)}, f32[18,512]{1,0:T(8,128)}, f32[1,18]{1,0:T(1,128)}, f32[18,512]{1,0:T(8,128)}) custom-call(f32[56,256]{1,0:T(8,128)S(1)} %add_add_fusion.mine_ref, f32[56,256]{1,0:T(8,128)S(1)} %collective-permute-done.11.other_ref), custom_call_target="tpu_custom_call" | custom-call | tf_op jit(solution)/shard_map/finish/pallas_call | solution.py:541
  (14 shorter events, 0.1 us)
Async XLA Ops:
  0.6 8.3 %copy-start = (bf16[18,512]{1,0:T(8,128)(2,1)S(1)}, bf16[18,512]{1,0:T(8,128)(2,1)}, u32[]{:S(2)}) copy-start(bf16[18,512]{1,0:T(8,128)(2,1)} %up_w_ref.3) | copy-start | bytes 55300
  3.7 9.7 %collective-permute-start = (bf16[2,24,1024]{2,1,0:T(8,128)(2,1)S(1)}, bf16[2,24,1024]{2,1,0:T(8,128)(2,1)S(1)}, u32[]{:S(2)}, u32[]{:S(2)}) collective-permute-start(bf16[2,24,1024]{2,1,0:T(8,128)(2,1)S(1)} %get-tuple-element.54), channel_id=1, source_target_pairs={{0,4},{4,0},{8,12},{12,8},{16,20},{20,16},{24,28},{28,24},{1,5},{5... | collective-permute-start | bytes 294920 | tf_op jit(solution)/shard_map/ppermute | solution.py:555
  4.3 9.2 %collective-permute-start.1 = (bf16[2,24,1024]{2,1,0:T(8,128)(2,1)S(1)}, bf16[2,24,1024]{2,1,0:T(8,128)(2,1)S(1)}, u32[]{:S(2)}, u32[]{:S(2)}) collective-permute-start(bf16[2,24,1024]{2,1,0:T(8,128)(2,1)S(1)} %get-tuple-element.55), channel_id=1, source_target_pairs={{0,28},{4,8},{8,4},{12,16},{16,12},{20,24},{24,20},{28,0},{1,29},{... | collective-permute-start | bytes 294920 | tf_op jit(solution)/shard_map/ppermute | solution.py:560
  13.5 7.1 %collective-permute-start.3 = (bf16[224,128]{1,0:T(8,128)(2,1)S(1)}, bf16[224,128]{1,0:T(8,128)(2,1)S(1)}, u32[]{:S(2)}, u32[]{:S(2)}) collective-permute-start(bf16[224,128]{1,0:T(8,128)(2,1)S(1)} %get-tuple-element.66), channel_id=1, source_target_pairs={{0,3},{1,2},{2,1},{3,0},{4,7},{5,6},{6,5},{7,4},{8,11},{9,10},{10,... | collective-permute-start | bytes 172040 | tf_op jit(solution)/shard_map/ppermute | solution.py:560
  16.0 4.6 %collective-permute-start.2 = (bf16[224,128]{1,0:T(8,128)(2,1)S(1)}, bf16[224,128]{1,0:T(8,128)(2,1)S(1)}, u32[]{:S(2)}, u32[]{:S(2)}) collective-permute-start(bf16[224,128]{1,0:T(8,128)(2,1)S(1)} %get-tuple-element.63.after), channel_id=1, source_target_pairs={{0,1},{1,0},{2,3},{3,2},{4,5},{5,4},{6,7},{7,6},{8,9},{9,8},{10,11... | collective-permute-start | bytes 172040 | tf_op jit(solution)/shard_map/ppermute | solution.py:555
  21.5 1.3 %collective-permute-start.4 = (f32[56,256]{1,0:T(8,128)S(1)}, f32[56,256]{1,0:T(8,128)S(1)}, u32[]{:S(2)}, u32[]{:S(2)}) collective-permute-start(f32[56,256]{1,0:T(8,128)S(1)} %get-tuple-element.74), channel_id=1, source_target_pairs={{0,4},{4,0},{8,12},{12,8},{16,20},{20,16},{24,28},{28,24},{1,5},{5... | collective-permute-start | bytes 172040 | tf_op jit(solution)/shard_map/ppermute | solution.py:555
  22.8 5.5 %collective-permute-start.7 = (f32[56,256]{1,0:T(8,128)S(1)}, f32[56,256]{1,0:T(8,128)S(1)}, u32[]{:S(2)}, u32[]{:S(2)}) collective-permute-start(f32[56,256]{1,0:T(8,128)S(1)} %add.21), channel_id=1, source_target_pairs={{0,16},{4,20},{8,24},{12,28},{16,0},{20,4},{24,8},{28,12},{1,17},{... | collective-permute-start | bytes 172040 | tf_op jit(solution)/shard_map/ppermute | solution.py:555
  22.9 5.4 %collective-permute-start.6 = (f32[56,256]{1,0:T(8,128)S(1)}, f32[56,256]{1,0:T(8,128)S(1)}, u32[]{:S(2)}, u32[]{:S(2)}) collective-permute-start(f32[56,256]{1,0:T(8,128)S(1)} %add.21), channel_id=1, source_target_pairs={{0,8},{4,12},{8,0},{12,4},{16,24},{20,28},{24,16},{28,20},{1,9},{5... | collective-permute-start | bytes 172040 | tf_op jit(solution)/shard_map/ppermute | solution.py:555
  24.2 6.1 %collective-permute-start.5 = (f32[56,256]{1,0:T(8,128)S(1)}, f32[56,256]{1,0:T(8,128)S(1)}, u32[]{:S(2)}, u32[]{:S(2)}) collective-permute-start(f32[56,256]{1,0:T(8,128)S(1)} %add.21), channel_id=1, source_target_pairs={{0,24},{4,28},{8,16},{12,20},{16,8},{20,12},{24,0},{28,4},{1,25},{... | collective-permute-start | bytes 172040 | tf_op jit(solution)/shard_map/ppermute | solution.py:555
  30.3 4.2 %collective-permute-start.8 = (f32[56,256]{1,0:T(8,128)S(1)}, f32[56,256]{1,0:T(8,128)S(1)}, u32[]{:S(2)}, u32[]{:S(2)}) collective-permute-start(f32[56,256]{1,0:T(8,128)S(1)} %add_add_fusion.1.refs_0_.refs_1_), channel_id=1, source_target_pairs={{0,2},{1,3},{2,0},{3,1},{4,6},{5,7},{6,4},{7,5},{8,10},{9,11},{10,... | collective-permute-start | bytes 172040 | tf_op jit(solution)/shard_map/ppermute | solution.py:555
  30.9 7.0 %collective-permute-start.10 = (f32[56,256]{1,0:T(8,128)S(1)}, f32[56,256]{1,0:T(8,128)S(1)}, u32[]{:S(2)}, u32[]{:S(2)}) collective-permute-start(f32[56,256]{1,0:T(8,128)S(1)} %add_add_fusion.1.refs_0_.refs_1_), channel_id=1, source_target_pairs={{0,3},{1,2},{2,1},{3,0},{4,7},{5,6},{6,5},{7,4},{8,11},{9,10},{10,... | collective-permute-start | bytes 172040 | tf_op jit(solution)/shard_map/ppermute | solution.py:555
  33.3 4.6 %collective-permute-start.9 = (f32[56,256]{1,0:T(8,128)S(1)}, f32[56,256]{1,0:T(8,128)S(1)}, u32[]{:S(2)}, u32[]{:S(2)}) collective-permute-start(f32[56,256]{1,0:T(8,128)S(1)} %add_add_fusion.1.refs_0_.refs_1_), channel_id=1, source_target_pairs={{0,1},{1,0},{2,3},{3,2},{4,5},{5,4},{6,7},{7,6},{8,9},{9,8},{10,11... | collective-permute-start | bytes 172040 | tf_op jit(solution)/shard_map/ppermute | solution.py:555
  38.0 1.4 %collective-permute-start.11 = (f32[56,256]{1,0:T(8,128)S(1)}, f32[56,256]{1,0:T(8,128)S(1)}, u32[]{:S(2)}, u32[]{:S(2)}) collective-permute-start(f32[56,256]{1,0:T(8,128)S(1)} %add_add_fusion.mine_ref), channel_id=1, source_target_pairs={{0,4},{4,0},{8,12},{12,8},{16,20},{20,16},{24,28},{28,24},{1,5},{5... | collective-permute-start | bytes 172040 | tf_op jit(solution)/shard_map/ppermute | solution.py:555
where the time goes:
time: 40.3 us; the launch traced here: 40.1 us
  Pallas kernels  17.8 us (44%)
  starting transfers between devices  16.4 us (41%)
  waiting for transfers between devices  4.99 us (12%)
  between operations  0.8 us (2%)
    ppermute x10, starting transfers between devices, swap(): lax.ppermute(x, axis, [(i, i ^ mask) for i in range(lax.axis_size(axis))])  9.23 us
    ppermute x2, starting transfers between devices, swap_outer(): lax.ppermute(x, axis, [(i, ((i + 1 ^ 1) - 1) % count) for i in range(coun...  7.21 us
    ppermute x10, waiting for transfers between devices, swap(): lax.ppermute(x, axis, [(i, i ^ mask) for i in range(lax.axis_size(axis))])  4.99 us
    pallas_call x1, Pallas kernels, middle(): pl.pallas_call(middle_kernel, in_specs=[HBM] * 2 + [VMEM] * 6, out_specs=...  4.43 us
    pallas_call x1, Pallas kernels, inner(): pl.pallas_call(inner_kernel, in_specs=[HBM] + [VMEM] * 10 + [pl.BlockSpec...  4.08 us
    pallas_call x1, Pallas kernels, back(): pl.pallas_call(functools.partial(back_kernel, count, slots), in_specs=[VM...  3.33 us
    pallas_call x1, Pallas kernels, encode(): pl.pallas_call(encode_kernel, in_specs=[HBM] * 3, out_specs=[VMEM] * 10,...  3.06 us
    pallas_call x1, Pallas kernels, store(): pl.pallas_call(store_kernel, in_specs=[VMEM, HBM], out_specs=HBM, out_sha...  1.34 us
  transfers between devices with their start and end apart: 12, of which 4 were waited for; matrix products, arithmetic and copies ran while one was open for 0% of the time, Pallas kernels for 33%

commit v1 on v0

--- a/solution.py
+++ b/solution.py
@@ -289,17 +289,14 @@
 
 
 def inner_kernel(
-    c_hbm, xe_ref, xa_ref, xm_ref, sqe_ref, sqm_ref, ha_a, ha_b, cg_in, up_in, up_w_ref, after,
+    c_ref, xe_ref, xa_ref, xm_ref, sqe_ref, sqm_ref, ha_a, ha_b, cg_in, up_in, up_w_ref, after,
     cg_ref, up_ref, g_ref, slope_ref, ent_ref, acc_ref, columns_ref, pe_ref,
-    c_ref, stacked, sem,
+    stacked,
 ):
-    late, bits, lanes = cg_ref.shape
+    _, bits, lanes = cg_ref.shape
     early, rows = cg_in.shape[0], g_ref.shape[0]
     images, width = xe_ref.shape[2:]
     edge = 2 * images
-    copies = [pltpu.make_async_copy(c_hbm.at[early + k], c_ref.at[k], sem.at[k]) for k in range(late)]
-    for copy in copies:
-        copy.start()
     ha_even = even("ha")
     stacked[...] = jnp.zeros_like(stacked)
     for k in range(2):
@@ -323,8 +320,7 @@
         if r < early:
             cg = cg_in[r]
         else:
-            copies[r - early].wait()
-            cg, total = outward_row(c_ref[r - early], up_w_ref[...], squash, total)
+            cg, total = outward_row(c_ref[r], up_w_ref[...], squash, total)
             cg_ref[r - early] = cg
         slope_row(r + 2)
         t = slope_ref[r] + slope_ref[r + 1] + slope_ref[r + 2]
@@ -338,13 +334,13 @@
 
 
 def inner(cotangent, x_edge, x_ahead, x_middle, sq_edge, sq_middle, ha_a, ha_b, cg, up, w_up, after):
-    rows, cols, images, width = cotangent.shape
+    rows, _, images, width = cotangent.shape
     early, bits, lanes = cg.shape
     late, edge = rows - early, 2 * images
     padded = -(-bits // 16) * 16
     return pl.pallas_call(
         inner_kernel,
-        in_specs=[HBM] + [VMEM] * 10 + [pl.BlockSpec(memory_space=pl.ANY)],
+        in_specs=[VMEM] * 11 + [pl.BlockSpec(memory_space=pl.ANY)],
         out_specs=[VMEM] * 8,
         out_shape=[
             spaced((late, bits, lanes)),
@@ -357,9 +353,7 @@
             spaced((rows + 4, bits, lanes)),
         ],
         scratch_shapes=[
-            pltpu.VMEM((late, cols, images, width), BF),
             pltpu.VMEM((2, 2 * padded, lanes - 2 * edge), BF),
-            pltpu.SemaphoreType.DMA((late,)),
         ],
         compiler_params=params(12),
         cost_estimate=cost(2 * (2 * late + rows) * lanes * width * 256, late * lanes * width * 2),
@@ -586,7 +580,7 @@
     early, first = EARLY_ROWS, FIRST_ROWS
     near = lambda a: pltpu.with_memory_space_constraint(a, pltpu.HBM)
     resident = lambda a: pltpu.with_memory_space_constraint(a, pltpu.VMEM)
-    latents, cotangent = near(latents), near(cotangent)
+    held, latents, cotangent = resident(cotangent), near(latents), near(cotangent)
     x_e, sq_e, ea_e, eb_e, ra, rb, mass, wt, bias, x_a = encode(latents, near(w_down.T), near(bit_bias.reshape(1, bits)), padded, AHEAD_ROWS)
     ha_b = swap_outer(rb, "ha")
     ha_a = swap(ra, "ha", 1)
@@ -594,7 +588,7 @@
     x_e, x_a, x_m = resident(x_e), resident(x_a), resident(x_m)
     ea, eb = pack((ea_e, eb_e, ea_m, eb_m), (ha_a, ha_b), mass, rows, bits)
     wa_a, wa_b = swap(ea, "wa", 1), swap_outer(eb, "wa")
-    cg1, up, g_inner, slope, ent_inner, acc, sums, probs = inner(cotangent, x_e, x_a, x_m, sq_e, sq_m, ha_a, ha_b, cg0, up, w_up, ea)
+    cg1, up, g_inner, slope, ent_inner, acc, sums, probs = inner(held, x_e, x_a, x_m, sq_e, sq_m, ha_a, ha_b, cg0, up, w_up, ea)
     g_outer, ent_outer, mine, other = outer(
         rows, width, images, x_e, x_a, x_m, sq_e, sq_m, cg0, cg1, wa_a, wa_b, slope, probs, acc, sums, up, mass
     )

time: 40.3 us -> 40.2 us (level)
  no operation moved by 1% of the time
where the time goes in v1:
time: 40.2 us; the launch traced here: 40 us
  Pallas kernels  17.8 us (44%)
  starting transfers between devices  16.4 us (41%)
  waiting for transfers between devices  4.91 us (12%)
  between operations  0.8 us (2%)
    ppermute x10, starting transfers between devices, swap(): lax.ppermute(x, axis, [(i, i ^ mask) for i in range(lax.axis_size(axis))])  9.24 us
    ppermute x2, starting transfers between devices, swap_outer(): lax.ppermute(x, axis, [(i, ((i + 1 ^ 1) - 1) % count) for i in range(coun...  7.21 us
    ppermute x10, waiting for transfers between devices, swap(): lax.ppermute(x, axis, [(i, i ^ mask) for i in range(lax.axis_size(axis))])  4.91 us
    pallas_call x1, Pallas kernels, middle(): pl.pallas_call(middle_kernel, in_specs=[HBM] * 2 + [VMEM] * 6, out_specs=...  4.58 us
    pallas_call x1, Pallas kernels, inner(): pl.pallas_call(inner_kernel, in_specs=[VMEM] * 11 + [pl.BlockSpec(memory_...  3.76 us
    pallas_call x1, Pallas kernels, back(): pl.pallas_call(functools.partial(back_kernel, count, slots), in_specs=[VM...  3.33 us
    pallas_call x1, Pallas kernels, encode(): pl.pallas_call(encode_kernel, in_specs=[HBM] * 3, out_specs=[VMEM] * 10,...  3.21 us
    pallas_call x1, Pallas kernels, store(): pl.pallas_call(store_kernel, in_specs=[VMEM, HBM], out_specs=HBM, out_sha...  1.34 us
  transfers between devices with their start and end apart: 12, of which 4 were waited for; matrix products, arithmetic and copies ran while one was open for 0% of the time, Pallas kernels for 33%

profile of v1, /device:TPU:0, one launch (start us, length us, event | category | flops | bytes accessed | tf_op | source)
XLA Modules:
  0.0 40.0 jit_solution(710454302999613687)
XLA Ops:
  0.6 0.0 slice-start
  0.7 3.2 %encode.1 = (bf16[4,16,64,512]{3,2,1,0:T(8,128)(2,1)S(1)}, f32[4,18,1024]{2,1,0:T(8,128)S(1)}, bf16[4,24,128]{2,1,0:T(8,128)(2,1)S(1)}, bf16[4,24,128]{2,1,0:T(8...) custom-call(bf16[8,16,64,512]{3,2,1,0:T(8,128)(2,1)} %x_hbm.3, ...), custom_call_target="tpu_custom_call" | custom-call | flops 1073741824 | bytes 4194304 | tf_op jit(solution)/shard_map/encode/pallas_call | solution.py:128
  3.9 0.6 %collective-permute-start = (bf16[2,24,1024]{2,1,0:T(8,128)(2,1)S(1)}, bf16[2,24,1024]{2,1,0:T(8,128)(2,1)S(1)}, u32[]{:S(2)}, u32[]{:S(2)}) collective-permute-start(bf16[2,24,1024]{2,1,0:T(8,128)(2,1)S(1)} %get-tuple-element.54), channel_id=1, source_target_pairs={{0,4},{4,0},{8,12},{12,8},{16,20},{20,16},{24,28},{28,24},{1,5},{5... | collective-permute-start | bytes 294920 | tf_op jit(solution)/shard_map/ppermute | solution.py:549
  4.4 4.7 %collective-permute-start.1 = (bf16[2,24,1024]{2,1,0:T(8,128)(2,1)S(1)}, bf16[2,24,1024]{2,1,0:T(8,128)(2,1)S(1)}, u32[]{:S(2)}, u32[]{:S(2)}) collective-permute-start(bf16[2,24,1024]{2,1,0:T(8,128)(2,1)S(1)} %get-tuple-element.55), channel_id=1, source_target_pairs={{0,28},{4,8},{8,4},{12,16},{16,12},{20,24},{24,20},{28,0},{1,29},{... | collective-permute-start | bytes 294920 | tf_op jit(solution)/shard_map/ppermute | solution.py:554
  9.1 4.6 %middle.1 = (bf16[2,16,64,512]{3,2,1,0:T(8,128)(2,1)S(1)}, f32[4,18,1024]{2,1,0:T(8,128)S(1)}, bf16[4,24,128]{2,1,0:T(8,128)(2,1)S(1)}, bf16[4,24,128]{2,1,0:T(8...) custom-call(bf16[8,16,64,512]{3,2,1,0:T(8,128)(2,1)} %x_hbm.3, ...), custom_call_target="tpu_custom_call" | custom-call | flops 3221225472 | bytes 8388608 | tf_op jit(solution)/shard_map/middle/pallas_call | solution.py:193
  13.8 2.5 %collective-permute-start.3 = (bf16[224,128]{1,0:T(8,128)(2,1)S(1)}, bf16[224,128]{1,0:T(8,128)(2,1)S(1)}, u32[]{:S(2)}, u32[]{:S(2)}) collective-permute-start(bf16[224,128]{1,0:T(8,128)(2,1)S(1)} %get-tuple-element.66), channel_id=1, source_target_pairs={{0,3},{1,2},{2,1},{3,0},{4,7},{5,6},{6,5},{7,4},{8,11},{9,10},{10,... | collective-permute-start | bytes 172040 | tf_op jit(solution)/shard_map/ppermute | solution.py:554
  16.3 0.5 %collective-permute-start.2 = (bf16[224,128]{1,0:T(8,128)(2,1)S(1)}, bf16[224,128]{1,0:T(8,128)(2,1)S(1)}, u32[]{:S(2)}, u32[]{:S(2)}) collective-permute-start(bf16[224,128]{1,0:T(8,128)(2,1)S(1)} %get-tuple-element.63.after), channel_id=1, source_target_pairs={{0,1},{1,0},{2,3},{3,2},{4,5},{5,4},{6,7},{7,6},{8,9},{9,8},{10,11... | collective-permute-start | bytes 172040 | tf_op jit(solution)/shard_map/ppermute | solution.py:549
  16.8 3.8 %inner.1 = (f32[4,18,1024]{2,1,0:T(8,128)S(1)}, f32[18,512]{1,0:T(8,128)S(1)}, f32[8,18,768]{2,1,0:T(8,128)S(1)}, f32[10,18,896]{2,1,0:T(8,128)S(1)}, f32[8,896]...) custom-call(bf16[8,16,64,512]{3,2,1,0:T(8,128)(2,1)S(1)} %bitcast.6, ...), custom_call_target="tpu_custom_call" | custom-call | flops 4294967296 | bytes 4194304 | tf_op jit(solution)/shard_map/inner/pallas_call | solution.py:341
  20.6 0.8 %outer.1 = (f32[8,18,256]{2,1,0:T(8,128)S(1)}, f32[8,128]{1,0:T(8,128)S(1)}, f32[56,256]{1,0:T(8,128)S(1)}, f32[56,256]{1,0:T(8,128)S(1)}) custom-call(bf16[4,16,64,512]{3,2,1,0:T(8,128)(2,1)S(1)} %get-tuple-element.46.xe_ref, bf16[2,16,64,512]{3,2,1,0:T(8,128)(2,1)S(1)} %get-tuple-element.47.xa_ref, bf16[2,16,64,512]{3,2,1,0:T(8,128)(2,1)S(1)} %get-tuple-element.52.xm_ref, ...), custom_call_target="tpu_custom_call" | custom-call | flops 536870912 | bytes 1048576 | tf_op jit(solution)/shard_map/outer/pallas_call | solution.py:429
  21.5 0.1 collective-permute-start.4
  21.5 1.2 %collective-permute-done.4 = f32[56,256]{1,0:T(8,128)S(1)} collective-permute-done((f32[56,256]{1,0:T(8,128)S(1)}, f32[56,256]{1,0:T(8,128)S(1)}, u32[]{:S(2)}, u32[]{:S(2)}) %collective-permute-start.4) | collective-permute-done | bytes 57376 | tf_op jit(solution)/shard_map/ppermute | solution.py:549
  22.8 0.1 collective-permute-start.7
  22.9 1.4 %collective-permute-start.6 = (f32[56,256]{1,0:T(8,128)S(1)}, f32[56,256]{1,0:T(8,128)S(1)}, u32[]{:S(2)}, u32[]{:S(2)}) collective-permute-start(f32[56,256]{1,0:T(8,128)S(1)} %add.21), channel_id=1, source_target_pairs={{0,8},{4,12},{8,0},{12,4},{16,24},{20,28},{24,16},{28,20},{1,9},{5... | collective-permute-start | bytes 172040 | tf_op jit(solution)/shard_map/ppermute | solution.py:549
  24.2 3.0 %collective-permute-start.5 = (f32[56,256]{1,0:T(8,128)S(1)}, f32[56,256]{1,0:T(8,128)S(1)}, u32[]{:S(2)}, u32[]{:S(2)}) collective-permute-start(f32[56,256]{1,0:T(8,128)S(1)} %add.21), channel_id=1, source_target_pairs={{0,24},{4,28},{8,16},{12,20},{16,8},{20,12},{24,0},{28,4},{1,25},{... | collective-permute-start | bytes 172040 | tf_op jit(solution)/shard_map/ppermute | solution.py:549
  27.2 1.1 %collective-permute-done.7 = f32[56,256]{1,0:T(8,128)S(1)} collective-permute-done((f32[56,256]{1,0:T(8,128)S(1)}, f32[56,256]{1,0:T(8,128)S(1)}, u32[]{:S(2)}, u32[]{:S(2)}) %collective-permute-start.7) | collective-permute-done | bytes 57376 | tf_op jit(solution)/shard_map/ppermute | solution.py:549
  28.3 1.9 %collective-permute-done.5 = f32[56,256]{1,0:T(8,128)S(1)} collective-permute-done((f32[56,256]{1,0:T(8,128)S(1)}, f32[56,256]{1,0:T(8,128)S(1)}, u32[]{:S(2)}, u32[]{:S(2)}) %collective-permute-start.5) | collective-permute-done | bytes 57376 | tf_op jit(solution)/shard_map/ppermute | solution.py:549
  30.2 0.6 %collective-permute-start.8 = (f32[56,256]{1,0:T(8,128)S(1)}, f32[56,256]{1,0:T(8,128)S(1)}, u32[]{:S(2)}, u32[]{:S(2)}) collective-permute-start(f32[56,256]{1,0:T(8,128)S(1)} %add_add_fusion.1.refs_0_.refs_1_), channel_id=1, source_target_pairs={{0,2},{1,3},{2,0},{3,1},{4,6},{5,7},{6,4},{7,5},{8,10},{9,11},{10,... | collective-permute-start | bytes 172040 | tf_op jit(solution)/shard_map/ppermute | solution.py:549
  30.8 2.4 %collective-permute-start.10 = (f32[56,256]{1,0:T(8,128)S(1)}, f32[56,256]{1,0:T(8,128)S(1)}, u32[]{:S(2)}, u32[]{:S(2)}) collective-permute-start(f32[56,256]{1,0:T(8,128)S(1)} %add_add_fusion.1.refs_0_.refs_1_), channel_id=1, source_target_pairs={{0,3},{1,2},{2,1},{3,0},{4,7},{5,6},{6,5},{7,4},{8,11},{9,10},{10,... | collective-permute-start | bytes 172040 | tf_op jit(solution)/shard_map/ppermute | solution.py:549
  33.2 0.6 %collective-permute-start.9 = (f32[56,256]{1,0:T(8,128)S(1)}, f32[56,256]{1,0:T(8,128)S(1)}, u32[]{:S(2)}, u32[]{:S(2)}) collective-permute-start(f32[56,256]{1,0:T(8,128)S(1)} %add_add_fusion.1.refs_0_.refs_1_), channel_id=1, source_target_pairs={{0,1},{1,0},{2,3},{3,2},{4,5},{5,4},{6,7},{7,6},{8,9},{9,8},{10,11... | collective-permute-start | bytes 172040 | tf_op jit(solution)/shard_map/ppermute | solution.py:549
  33.8 0.7 %collective-permute-done.8.refs_2_ = f32[56,256]{1,0:T(8,128)S(1)} collective-permute-done((f32[56,256]{1,0:T(8,128)S(1)}, f32[56,256]{1,0:T(8,128)S(1)}, u32[]{:S(2)}, u32[]{:S(2)}) %collective-permute-start.8) | collective-permute-done | bytes 57376 | tf_op jit(solution)/shard_map/ppermute | solution.py:549
  34.5 3.3 %back.1 = (bf16[8,16,64,512]{3,2,1,0:T(8,128)(2,1)}, f32[8,16,64]{2,1,0:T(8,128)}, bf16[2,16,64,512]{3,2,1,0:T(8,128)(2,1)S(1)}) custom-call(f32[8,18,768]{2,1,0:T(8,128)S(1)} %get-tuple-element.64.gi_ref, f32[8,18,256]{2,1,0:T(8,128)S(1)} %get-tuple-element.72.go_ref, f32[4,18,1024]{2,1,0:T(8,128)S(1)} %get-tuple-element.50.sqe_ref, ...), custom_call_target="tpu_custom_call" | custom-call | flops 2147483648 | bytes 8388608 | tf_op jit(solution)/shard_map/back/pallas_call | solution.py:476
  37.9 0.1 collective-permute-start.11
  37.9 1.3 %store.1 = bf16[8,16,64,512]{3,2,1,0:T(8,128)(2,1)} custom-call(bf16[2,16,64,512]{3,2,1,0:T(8,128)(2,1)S(1)} %get-tuple-element.77.rest_ref, bf16[8,16,64,512]{3,2,1,0:T(8,128)(2,1)} %get-tuple-element.79._), custom_call_target="tpu_custom_call", output_to_operand_aliasing={{}: (1, {})} | custom-call | bytes 2097152 | tf_op jit(solution)/shard_map/store/pallas_call | solution.py:504
  39.3 0.7 %finish.1 = (f32[1,18]{1,0:T(1,128)}, f32[18,512]{1,0:T(8,128)}, f32[1,18]{1,0:T(1,128)}, f32[18,512]{1,0:T(8,128)}) custom-call(f32[56,256]{1,0:T(8,128)S(1)} %add_add_fusion.mine_ref, f32[56,256]{1,0:T(8,128)S(1)} %collective-permute-done.11.other_ref), custom_call_target="tpu_custom_call" | custom-call | tf_op jit(solution)/shard_map/finish/pallas_call | solution.py:535
  (19 shorter events, 0.1 us)
Async XLA Ops:
  0.6 8.5 %copy-start = (bf16[18,512]{1,0:T(8,128)(2,1)S(1)}, bf16[18,512]{1,0:T(8,128)(2,1)}, u32[]{:S(2)}) copy-start(bf16[18,512]{1,0:T(8,128)(2,1)} %up_w_ref.3) | copy-start | bytes 55300
  0.6 16.2 %slice-start = ((s8[8388608]{0:T(1024)(128)(4,1)}), s8[4194304]{0:T(1024)(128)(4,1)S(1)}, s32[]{:S(2)}) async-start(s8[8388608]{0:T(1024)(128)(4,1)} %bitcast.5), calls=%async_computation | async-start | bytes 8388608
  3.9 9.9 %collective-permute-start = (bf16[2,24,1024]{2,1,0:T(8,128)(2,1)S(1)}, bf16[2,24,1024]{2,1,0:T(8,128)(2,1)S(1)}, u32[]{:S(2)}, u32[]{:S(2)}) collective-permute-start(bf16[2,24,1024]{2,1,0:T(8,128)(2,1)S(1)} %get-tuple-element.54), channel_id=1, source_target_pairs={{0,4},{4,0},{8,12},{12,8},{16,20},{20,16},{24,28},{28,24},{1,5},{5... | collective-permute-start | bytes 294920 | tf_op jit(solution)/shard_map/ppermute | solution.py:549
  4.4 9.3 %collective-permute-start.1 = (bf16[2,24,1024]{2,1,0:T(8,128)(2,1)S(1)}, bf16[2,24,1024]{2,1,0:T(8,128)(2,1)S(1)}, u32[]{:S(2)}, u32[]{:S(2)}) collective-permute-start(bf16[2,24,1024]{2,1,0:T(8,128)(2,1)S(1)} %get-tuple-element.55), channel_id=1, source_target_pairs={{0,28},{4,8},{8,4},{12,16},{16,12},{20,24},{24,20},{28,0},{1,29},{... | collective-permute-start | bytes 294920 | tf_op jit(solution)/shard_map/ppermute | solution.py:554
  9.1 7.7 %slice-start.1 = ((s8[8388608]{0:T(1024)(128)(4,1)}), s8[4194304]{0:T(1024)(128)(4,1)S(1)}, s32[]{:S(2)}) async-start(s8[8388608]{0:T(1024)(128)(4,1)} %bitcast.5), calls=%async_computation.1 | async-start | bytes 8388608
  13.8 6.8 %collective-permute-start.3 = (bf16[224,128]{1,0:T(8,128)(2,1)S(1)}, bf16[224,128]{1,0:T(8,128)(2,1)S(1)}, u32[]{:S(2)}, u32[]{:S(2)}) collective-permute-start(bf16[224,128]{1,0:T(8,128)(2,1)S(1)} %get-tuple-element.66), channel_id=1, source_target_pairs={{0,3},{1,2},{2,1},{3,0},{4,7},{5,6},{6,5},{7,4},{8,11},{9,10},{10,... | collective-permute-start | bytes 172040 | tf_op jit(solution)/shard_map/ppermute | solution.py:554
  16.3 4.3 %collective-permute-start.2 = (bf16[224,128]{1,0:T(8,128)(2,1)S(1)}, bf16[224,128]{1,0:T(8,128)(2,1)S(1)}, u32[]{:S(2)}, u32[]{:S(2)}) collective-permute-start(bf16[224,128]{1,0:T(8,128)(2,1)S(1)} %get-tuple-element.63.after), channel_id=1, source_target_pairs={{0,1},{1,0},{2,3},{3,2},{4,5},{5,4},{6,7},{7,6},{8,9},{9,8},{10,11... | collective-permute-start | bytes 172040 | tf_op jit(solution)/shard_map/ppermute | solution.py:549
  21.5 1.3 %collective-permute-start.4 = (f32[56,256]{1,0:T(8,128)S(1)}, f32[56,256]{1,0:T(8,128)S(1)}, u32[]{:S(2)}, u32[]{:S(2)}) collective-permute-start(f32[56,256]{1,0:T(8,128)S(1)} %get-tuple-element.74), channel_id=1, source_target_pairs={{0,4},{4,0},{8,12},{12,8},{16,20},{20,16},{24,28},{28,24},{1,5},{5... | collective-permute-start | bytes 172040 | tf_op jit(solution)/shard_map/ppermute | solution.py:549
  22.8 5.5 %collective-permute-start.7 = (f32[56,256]{1,0:T(8,128)S(1)}, f32[56,256]{1,0:T(8,128)S(1)}, u32[]{:S(2)}, u32[]{:S(2)}) collective-permute-start(f32[56,256]{1,0:T(8,128)S(1)} %add.21), channel_id=1, source_target_pairs={{0,16},{4,20},{8,24},{12,28},{16,0},{20,4},{24,8},{28,12},{1,17},{... | collective-permute-start | bytes 172040 | tf_op jit(solution)/shard_map/ppermute | solution.py:549
  22.9 5.4 %collective-permute-start.6 = (f32[56,256]{1,0:T(8,128)S(1)}, f32[56,256]{1,0:T(8,128)S(1)}, u32[]{:S(2)}, u32[]{:S(2)}) collective-permute-start(f32[56,256]{1,0:T(8,128)S(1)} %add.21), channel_id=1, source_target_pairs={{0,8},{4,12},{8,0},{12,4},{16,24},{20,28},{24,16},{28,20},{1,9},{5... | collective-permute-start | bytes 172040 | tf_op jit(solution)/shard_map/ppermute | solution.py:549
  24.2 6.0 %collective-permute-start.5 = (f32[56,256]{1,0:T(8,128)S(1)}, f32[56,256]{1,0:T(8,128)S(1)}, u32[]{:S(2)}, u32[]{:S(2)}) collective-permute-start(f32[56,256]{1,0:T(8,128)S(1)} %add.21), channel_id=1, source_target_pairs={{0,24},{4,28},{8,16},{12,20},{16,8},{20,12},{24,0},{28,4},{1,25},{... | collective-permute-start | bytes 172040 | tf_op jit(solution)/shard_map/ppermute | solution.py:549
  30.2 4.2 %collective-permute-start.8 = (f32[56,256]{1,0:T(8,128)S(1)}, f32[56,256]{1,0:T(8,128)S(1)}, u32[]{:S(2)}, u32[]{:S(2)}) collective-permute-start(f32[56,256]{1,0:T(8,128)S(1)} %add_add_fusion.1.refs_0_.refs_1_), channel_id=1, source_target_pairs={{0,2},{1,3},{2,0},{3,1},{4,6},{5,7},{6,4},{7,5},{8,10},{9,11},{10,... | collective-permute-start | bytes 172040 | tf_op jit(solution)/shard_map/ppermute | solution.py:549
  30.8 7.0 %collective-permute-start.10 = (f32[56,256]{1,0:T(8,128)S(1)}, f32[56,256]{1,0:T(8,128)S(1)}, u32[]{:S(2)}, u32[]{:S(2)}) collective-permute-start(f32[56,256]{1,0:T(8,128)S(1)} %add_add_fusion.1.refs_0_.refs_1_), channel_id=1, source_target_pairs={{0,3},{1,2},{2,1},{3,0},{4,7},{5,6},{6,5},{7,4},{8,11},{9,10},{10,... | collective-permute-start | bytes 172040 | tf_op jit(solution)/shard_map/ppermute | solution.py:549
  33.2 4.7 %collective-permute-start.9 = (f32[56,256]{1,0:T(8,128)S(1)}, f32[56,256]{1,0:T(8,128)S(1)}, u32[]{:S(2)}, u32[]{:S(2)}) collective-permute-start(f32[56,256]{1,0:T(8,128)S(1)} %add_add_fusion.1.refs_0_.refs_1_), channel_id=1, source_target_pairs={{0,1},{1,0},{2,3},{3,2},{4,5},{5,4},{6,7},{7,6},{8,9},{9,8},{10,11... | collective-permute-start | bytes 172040 | tf_op jit(solution)/shard_map/ppermute | solution.py:549
  37.9 1.4 %collective-permute-start.11 = (f32[56,256]{1,0:T(8,128)S(1)}, f32[56,256]{1,0:T(8,128)S(1)}, u32[]{:S(2)}, u32[]{:S(2)}) collective-permute-start(f32[56,256]{1,0:T(8,128)S(1)} %add_add_fusion.mine_ref), channel_id=1, source_target_pairs={{0,4},{4,0},{8,12},{12,8},{16,20},{20,16},{24,28},{28,24},{1,5},{5... | collective-permute-start | bytes 172040 | tf_op jit(solution)/shard_map/ppermute | solution.py:549
